TPU v7x, 32 devices: a whole 2x2x4 slice. The times are simulated.
32 devices in a mesh: dp: 16 (over z, y, x), tensor: 2 (over core).
Axes of the slice: x: 2, y: 2, z: 4, core: 2. Of those that a mesh axis runs over, the one named last changes fastest.
Arguments:
- tokens: bfloat16 [2048, 1536], P('dp'), may hold values from -8 to 8
- attn_norm_gain: bfloat16 [1536], P('dp'), may hold values from 0.5 to 1.5
- w_query: bfloat16 [1536, 1536], P('dp', 'tensor'), may hold values from -1 to 1
- key_projection: bfloat16 [1536, 512], P('dp', 'tensor'), may hold values from -0.625 to 0.625
- value_projection: bfloat16 [1536, 512], P('dp', 'tensor'), may hold values from -0.15625 to 0.15625
- w_out: bfloat16 [1536, 1536], P('dp', 'tensor'), may hold values from -2 to 2
- moe_norm_gain: bfloat16 [1536], P('dp'), may hold values from 0.5 to 1.5
- w_gate: bfloat16 [16, 1536, 512], P('dp', None, 'tensor'), may hold values from -0.15625 to 0.15625
- w_up: bfloat16 [16, 1536, 512], P('dp', None, 'tensor'), may hold values from -0.15625 to 0.15625
- w_down: bfloat16 [16, 1536, 512], P('dp', None, 'tensor'), may hold values from -4 to 4
- router_logits: float32 [2048, 8], P('dp'), may hold values from -3 to 3
- expert_ids: int32 [2048, 8], P('dp'), may hold values from 0 to 15, all different within a row; in each aligned block of 128 rows (0 to 127, 128 to 255, ...) at most 72 rows name the same one
- segment_ids: int32 [16, 128], P('dp'), may hold values from 0 to 12, never falling along the last dimension, each value on 1 to 32 neighbouring positions
- parents: int32 [16, 13], P('dp'), may hold values from 0 to 4, as said below
- cotangent: bfloat16 [2048, 1536], P('dp'), may hold values from -6 to 6
Outputs:
- output: bfloat16 [2048, 1536], P('dp')
- input_grad: float32 [2048, 1536], P('dp')
- grad_attn_norm_gain: float32 [1536], P('dp')
- grad_w_query: float32 [1536, 1536], P('dp', 'tensor')
- grad_w_key: float32 [1536, 512], P('dp', 'tensor')
- grad_w_value: float32 [1536, 512], P('dp', 'tensor')
- grad_w_out: float32 [1536, 1536], P('dp', 'tensor')
- grad_moe_norm_gain: float32 [1536], P('dp')
- grad_w_gate: float32 [16, 1536, 512], P('dp', None, 'tensor')
- grad_w_up: float32 [16, 1536, 512], P('dp', None, 'tensor')
- grad_w_down: float32 [16, 1536, 512], P('dp', None, 'tensor')
- clipped_w_query: float32 [1536, 1536], P('dp', 'tensor')
- clipped_w_key: float32 [1536, 512], P('dp', 'tensor')
Inputs may be any that keep to these rules, and one draw needn't show every extreme that they name: `expert_ids`: each row names 8 different experts; within the rows of one tree no expert is named by more than 72 rows, a bound that some block reaches. `segment_ids`: along a tree the segment numbers never fall; each segment has 1 to 32 tokens, one exactly 32. `parents`: segment 0 is the trunk and its own parent; segments 1 to 4 have parent 0; every later segment has a parent among 1 to 4.
All inputs are finite; a program needn't handle non-finite values.
Results may differ from a plain program's by a relative error of at most 0.017.
Values may be sent and summed in bfloat16 or wider, within the bound.
A program may use at most 384 MiB of HBM per device.

v0:
```python
import functools
import types

import jax
import jax.numpy as jnp
from jax import lax
from jax.experimental import pallas as pl
from jax.experimental.pallas import tpu as pltpu
from jax.sharding import PartitionSpec as P

HEAD_SIZE = 64
FFE = 512
TOP = 8


EPSILON = 1e-06
SCORE_SCALE = 1.0 / 64.0
RESIDUAL = 0.22
THETA = 10000.0
CLIP_LIMIT = 2.0
NEGATIVE = -1e30


def tree_layout(seg_row, par_row):
    tree_length = seg_row.shape[0]
    seg_count = par_row.shape[0]
    seg_index = jnp.arange(seg_count, dtype=jnp.int32)
    member = (seg_row[:, None] == seg_index[None, :]).astype(jnp.int32)
    seg_len = jnp.sum(member, axis=0)
    seg_start = jnp.sum(jnp.where(seg_index[:, None] > seg_index[None, :], seg_len[None, :], 0), axis=1)
    parent_hot = (par_row[:, None] == seg_index[None, :]).astype(jnp.int32)
    grand_parent = jnp.sum(parent_hot * par_row[None, :], axis=1)
    grand_hot = (grand_parent[:, None] == seg_index[None, :]).astype(jnp.int32)
    parent_len = jnp.sum(parent_hot * seg_len[None, :], axis=1)
    grand_len = jnp.sum(grand_hot * seg_len[None, :], axis=1)
    offset = jnp.where(seg_index != 0, parent_len, 0) + jnp.where(par_row != 0, grand_len, 0)
    tok_start = jnp.sum(member * seg_start[None, :], axis=1)
    tok_offset = jnp.sum(member * offset[None, :], axis=1)
    places = jnp.arange(tree_length, dtype=jnp.int32)
    position = (places - tok_start + tok_offset).astype(jnp.float32)
    identity = (seg_index[:, None] == seg_index[None, :]).astype(jnp.int32)
    ancestor = jnp.minimum(identity + parent_hot + grand_hot, 1)
    reached = jnp.dot(member, ancestor)
    linked = jnp.dot(reached, member.T) > 0
    allowed = linked & (places[None, :] <= places[:, None])
    return (position, allowed)


def rope_tables(position, head_dim):
    half_dim = head_dim // 2
    frequency = THETA ** (-2.0 * jnp.arange(half_dim, dtype=jnp.float32) / head_dim)
    angles = position[:, None] * frequency[None, :]
    return (jnp.cos(angles)[:, None, :], jnp.sin(angles)[:, None, :])


def apply_rotary(values_in, cosine_table, sine_values):
    half_dim = values_in.shape[-1] // 2
    first_half = values_in[..., :half_dim]
    second_half = values_in[..., half_dim:]
    return jnp.concatenate(
        [
            first_half * cosine_table - second_half * sine_values,
            second_half * cosine_table + first_half * sine_values,
        ],
        axis=-1,
    )


def rotate_back(grads_in, cosine_table, sine_values):
    half_dim = grads_in.shape[-1] // 2
    first_half = grads_in[..., :half_dim]
    second_half = grads_in[..., half_dim:]
    return jnp.concatenate(
        [
            first_half * cosine_table + second_half * sine_values,
            second_half * cosine_table - first_half * sine_values,
        ],
        axis=-1,
    )


def slot_tables(routes, experts, capacity):
    flat_ids = routes.reshape(-1)
    row_count = flat_ids.shape[0]
    member = (flat_ids[:, None] == jnp.arange(experts, dtype=jnp.int32)[None, :]).astype(jnp.int32)
    row_total = flat_ids.shape[0]
    before = jnp.dot((jnp.arange(row_total)[:, None] > jnp.arange(row_total)[None, :]).astype(jnp.float32), member.astype(jnp.float32), precision=lax.Precision.HIGHEST).astype(jnp.int32)
    slot_index = jnp.sum(before * member, axis=1)
    target = flat_ids * capacity + slot_index
    source = (
        jnp.full((experts * capacity,), -1, jnp.int32)
        .at[target]
        .set(jnp.arange(row_count, dtype=jnp.int32))
    )
    return (flat_ids, slot_index, source)


def contract_rows(left, right):
    return lax.dot_general(
        left, right, (((0,), (0,)), ((), ())), preferred_element_type=jnp.float32
    )


def contract_cols(left, right):
    return lax.dot_general(
        left, right, (((1,), (1,)), ((), ())), preferred_element_type=jnp.float32
    )


def expert_forward(inputs, gate_w, up_w, down_w):
    gate_pre = jnp.dot(inputs, gate_w, preferred_element_type=jnp.float32)
    up_pre = jnp.dot(inputs, up_w, preferred_element_type=jnp.float32)
    active = (gate_pre / (1.0 + jnp.exp(-gate_pre)) * up_pre).astype(jnp.bfloat16)
    return (contract_cols(active, down_w), (gate_pre, up_pre, active))


def expert_backward(inputs, grads_out, gate_w, up_w, down_w, kept_acts):
    gate_pre, up_pre, active = kept_acts
    d_active = jnp.dot(grads_out, down_w, preferred_element_type=jnp.float32)
    grad_down = contract_rows(grads_out, active)
    sigmoid_val = 1.0 / (1.0 + jnp.exp(-gate_pre))
    d_gate = (d_active * up_pre * sigmoid_val * (1.0 + gate_pre * (1.0 - sigmoid_val))).astype(
        jnp.bfloat16
    )
    d_up = (d_active * gate_pre * sigmoid_val).astype(jnp.bfloat16)
    grad_gate = contract_rows(inputs, d_gate)
    grad_up = contract_rows(inputs, d_up)
    d_inputs = contract_cols(d_gate, gate_w) + contract_cols(d_up, up_w)
    return (d_inputs, grad_gate, grad_up, grad_down)


def send_rows(rows_in):
    return lax.all_to_all(rows_in, "dp", split_axis=0, concat_axis=0, tiled=True)


def return_rows(rows_in):
    return lax.all_to_all(
        rows_in.astype(jnp.bfloat16), "dp", split_axis=0, concat_axis=0, tiled=True
    ).astype(rows_in.dtype)


def send_grads(rows_in):
    return lax.all_to_all(rows_in, "dp", split_axis=0, concat_axis=0, tiled=True)


def return_grads(rows_in):
    return lax.all_to_all(
        rows_in.astype(jnp.bfloat16), "dp", split_axis=0, concat_axis=0, tiled=True
    ).astype(rows_in.dtype)


def share_slots(partial_rows):
    return lax.psum_scatter(partial_rows, "tensor", scatter_dimension=1, tiled=True)


def on_device_general(
    tokens,
    attn_norm_gain,
    w_query,
    key_projection,
    value_projection,
    w_out,
    moe_norm_gain,
    w_gate,
    w_up,
    w_down,
    router_logits,
    expert_ids,
    segment_ids,
    parents,
    cotangent,
):
    length = tokens.shape[0]
    model_width = tokens.shape[1]
    q_cols = w_query.shape[1]
    kv_cols = key_projection.shape[1]
    q_heads = q_cols // HEAD_SIZE
    kv_heads = kv_cols // HEAD_SIZE
    group_size = q_heads // kv_heads
    dp_size = lax.axis_size("dp")
    tensor_ranks = lax.axis_size("tensor")
    replicas = FFE // (w_gate.shape[2] * tensor_ranks)
    experts = dp_size // replicas
    capacity = 4 * (9 * length * TOP // (32 * experts))
    share_rows = capacity // tensor_ranks
    first_slot = lax.axis_index("tensor") * share_rows
    block_rows = min(length, 512)
    attn_gain, moe_gain, query_w, key_weight, value_weight, out_w = (
        lax.all_gather(attn_norm_gain, "dp", axis=0, tiled=True),
        lax.all_gather(moe_norm_gain, "dp", axis=0, tiled=True),
        lax.all_gather(w_query, "dp", axis=0, tiled=True),
        lax.all_gather(key_projection, "dp", axis=0, tiled=True),
        lax.all_gather(value_projection, "dp", axis=0, tiled=True),
        lax.all_gather(w_out, "dp", axis=0, tiled=True),
    )
    attn_gain_f = attn_gain.astype(jnp.float32)
    moe_gain_f = moe_gain.astype(jnp.float32)
    inputs = tokens.astype(jnp.float32)
    inv_attn = lax.rsqrt(jnp.mean(inputs * inputs, axis=1, keepdims=True) + EPSILON)
    unit_attn = inputs * inv_attn
    normalized_rows = (unit_attn * attn_gain_f).astype(jnp.bfloat16)
    position, allowed = tree_layout(segment_ids[0], parents[0])
    cosine_table, sine_values = rope_tables(position, HEAD_SIZE)
    query_linear = jnp.dot(normalized_rows, query_w, preferred_element_type=jnp.float32).reshape(
        length, q_heads, HEAD_SIZE
    )
    key_linear = jnp.dot(normalized_rows, key_weight, preferred_element_type=jnp.float32).reshape(
        length, kv_heads, HEAD_SIZE
    )
    query_heads = (
        apply_rotary(query_linear, cosine_table, sine_values)
        .astype(jnp.bfloat16)
        .reshape(length, kv_heads, group_size, HEAD_SIZE)
    )
    key_heads = apply_rotary(key_linear, cosine_table, sine_values).astype(jnp.bfloat16)
    value_heads = (
        jnp.dot(normalized_rows, value_weight, preferred_element_type=jnp.float32)
        .astype(jnp.bfloat16)
        .reshape(length, kv_heads, HEAD_SIZE)
    )
    q_block = query_heads
    mask_rows = allowed[None, None]
    scores = (
        jnp.einsum("qhgd,khd->hgqk", q_block, key_heads, preferred_element_type=jnp.float32)
        * SCORE_SCALE
    )
    scores = jnp.where(mask_rows, scores, NEGATIVE)
    peak_parts = [jnp.max(scores, axis=(2, 3))]
    row_max = jnp.max(scores, axis=3, keepdims=True)
    expo = jnp.exp(scores - row_max)
    row_total = jnp.sum(expo, axis=3, keepdims=True)
    lse_parts = [row_max + jnp.log(row_total)]
    prob_low = (expo / row_total).astype(jnp.bfloat16)
    block_outs = jnp.einsum(
        "hgqk,khd->qhgd", prob_low, value_heads, preferred_element_type=jnp.float32
    )
    head_out = block_outs.reshape(length, q_cols).astype(jnp.bfloat16)
    attn_mix = lax.psum(contract_cols(head_out, out_w), "tensor")
    hidden = inputs + RESIDUAL * attn_mix
    head_peak = lax.pmax(jnp.max(jnp.stack(peak_parts), axis=0).reshape(q_heads), "dp")
    inv_moe = lax.rsqrt(jnp.mean(hidden * hidden, axis=1, keepdims=True) + EPSILON)
    unit_moe = hidden * inv_moe
    moe_in = (unit_moe * moe_gain_f).astype(jnp.bfloat16)
    logit_max = jnp.max(router_logits, axis=1, keepdims=True)
    logit_exp = jnp.exp(router_logits - logit_max)
    gate_probs = logit_exp / jnp.sum(logit_exp, axis=1, keepdims=True)
    flat_ids, slot_index, source = slot_tables(expert_ids, experts, capacity)
    filled = source >= 0
    source_row = jnp.maximum(source, 0)
    source_token = source_row // TOP
    dispatch_rows = jnp.where(
        filled[:, None], moe_in[source_token], jnp.zeros((), jnp.bfloat16)
    ).reshape(experts, capacity, model_width)
    arrived = send_rows(jnp.repeat(dispatch_rows, replicas, axis=0))
    gate_w, up_w, down_w = (w_gate[0], w_up[0], w_down[0])
    expert_in = arrived.reshape(dp_size * capacity, model_width)
    expert_out, kept_acts = expert_forward(expert_in, gate_w, up_w, down_w)
    partial_out = share_slots(expert_out.reshape(dp_size, capacity, model_width))
    back_parts = return_rows(partial_out).reshape(experts, replicas, share_rows, model_width)
    back_rows = (
        jnp.sum(back_parts, axis=1).astype(jnp.bfloat16).reshape(experts * share_rows, model_width)
    )
    own_slot = ((slot_index >= first_slot) & (slot_index < first_slot + share_rows)).reshape(
        length, TOP
    )
    local_index = (
        flat_ids * share_rows + jnp.clip(slot_index - first_slot, 0, share_rows - 1)
    ).reshape(length, TOP)
    mix_part = jnp.zeros((length, model_width), jnp.float32)
    for column in range(TOP):
        gate_weight = jnp.where(own_slot[:, column], gate_probs[:, column], 0.0)
        mix_part = mix_part + gate_weight[:, None] * back_rows[local_index[:, column]].astype(
            jnp.float32
        )
    expert_mix = lax.psum(mix_part.astype(jnp.bfloat16), "tensor").astype(jnp.float32)
    output = (hidden + RESIDUAL * expert_mix).astype(jnp.bfloat16)
    grad_output = cotangent.astype(jnp.float32)
    mix_grad = RESIDUAL * grad_output
    row_gate = gate_probs.reshape(-1)[source_row]
    grad_rows = (
        jnp.where(filled[:, None], row_gate[:, None] * mix_grad[source_token], 0.0)
        .astype(jnp.bfloat16)
        .reshape(experts, capacity, model_width)
    )
    grad_arrived = send_grads(jnp.repeat(grad_rows, replicas, axis=0)).reshape(
        dp_size * capacity, model_width
    )
    d_inputs, grad_gate, grad_up, grad_down = expert_backward(
        expert_in, grad_arrived, gate_w, up_w, down_w, kept_acts
    )
    d_back = share_slots(d_inputs.reshape(dp_size, capacity, model_width))
    grad_gate, grad_up, grad_down = (grad_gate[None], grad_up[None], grad_down[None])
    d_parts = return_grads(d_back).reshape(experts, replicas, share_rows, model_width)
    d_returned = (
        jnp.sum(d_parts, axis=1).astype(jnp.bfloat16).reshape(experts * share_rows, model_width)
    )
    d_mix_part = jnp.zeros((length, model_width), jnp.float32)
    for column in range(TOP):
        d_mix_part = d_mix_part + jnp.where(
            own_slot[:, column][:, None],
            d_returned[local_index[:, column]].astype(jnp.float32),
            0.0,
        )
    d_moe_in = lax.psum(d_mix_part, "tensor")
    scaled_moe = d_moe_in * moe_gain_f
    grad_moe_gain = jnp.sum(d_moe_in * unit_moe, axis=0)
    d_hidden = grad_output + inv_moe * (
        scaled_moe - unit_moe * jnp.mean(scaled_moe * unit_moe, axis=1, keepdims=True)
    )
    d_attn = (RESIDUAL * d_hidden).astype(jnp.bfloat16)
    grad_out_w = contract_rows(d_attn, head_out)
    d_heads = (
        jnp.dot(d_attn, out_w, preferred_element_type=jnp.float32)
        .astype(jnp.bfloat16)
        .reshape(length, kv_heads, group_size, HEAD_SIZE)
    )
    d_query_parts = []
    d_key = jnp.zeros((length, kv_heads, HEAD_SIZE), jnp.float32)
    d_value = jnp.zeros((length, kv_heads, HEAD_SIZE), jnp.float32)
    for block_number, row_begin in enumerate(range(0, length, block_rows)):
        q_block = query_heads
        mask_rows = allowed[None, None]
        scores = (
            jnp.einsum("qhgd,khd->hgqk", q_block, key_heads, preferred_element_type=jnp.float32)
            * SCORE_SCALE
        )
        scores = jnp.where(mask_rows, scores, NEGATIVE)
        prob_full = jnp.exp(scores - lse_parts[block_number])
        prob_low = prob_full.astype(jnp.bfloat16)
        d_value = jnp.einsum(
            "hgqk,qhgd->khd", prob_low, d_heads, preferred_element_type=jnp.float32
        )
        d_prob = jnp.einsum(
            "qhgd,khd->hgqk", d_heads, value_heads, preferred_element_type=jnp.float32
        )
        inner = jnp.sum(prob_full * d_prob, axis=3, keepdims=True)
        d_scores = (prob_full * (d_prob - inner)).astype(jnp.bfloat16)
        d_query_parts.append(
            jnp.einsum("hgqk,khd->qhgd", d_scores, key_heads, preferred_element_type=jnp.float32)
            * SCORE_SCALE
        )
        d_key = (
            jnp.einsum("hgqk,qhgd->khd", d_scores, q_block, preferred_element_type=jnp.float32)
            * SCORE_SCALE
        )
    d_query_all = d_query_parts[0].reshape(length, q_heads, HEAD_SIZE)
    d_query_lin = (
        rotate_back(d_query_all, cosine_table, sine_values)
        .astype(jnp.bfloat16)
        .reshape(length, q_cols)
    )
    d_key_lin = (
        rotate_back(d_key, cosine_table, sine_values).astype(jnp.bfloat16).reshape(length, kv_cols)
    )
    d_value_lin = d_value.astype(jnp.bfloat16).reshape(length, kv_cols)
    grad_query_w = contract_rows(normalized_rows, d_query_lin)
    grad_key_w = contract_rows(normalized_rows, d_key_lin)
    grad_value_w = contract_rows(normalized_rows, d_value_lin)
    d_normed_part = (
        contract_cols(d_query_lin, query_w)
        + contract_cols(d_key_lin, key_weight)
        + contract_cols(d_value_lin, value_weight)
    )
    d_normed = lax.psum(d_normed_part.astype(jnp.bfloat16), "tensor").astype(jnp.float32)
    scaled_attn = d_normed * attn_gain_f
    grad_attn_gain = jnp.sum(d_normed * unit_attn, axis=0)
    input_grad = d_hidden + inv_attn * (
        scaled_attn - unit_attn * jnp.mean(scaled_attn * unit_attn, axis=1, keepdims=True)
    )
    reduced = (
        lax.psum_scatter(grad_attn_gain, "dp", scatter_dimension=0, tiled=True),
        lax.psum_scatter(grad_moe_gain, "dp", scatter_dimension=0, tiled=True),
        lax.psum_scatter(grad_query_w, "dp", scatter_dimension=0, tiled=True),
        lax.psum_scatter(grad_key_w, "dp", scatter_dimension=0, tiled=True),
        lax.psum_scatter(grad_value_w, "dp", scatter_dimension=0, tiled=True),
        lax.psum_scatter(grad_out_w, "dp", scatter_dimension=0, tiled=True),
    )
    scale_factor = CLIP_LIMIT / jnp.maximum(head_peak, CLIP_LIMIT)
    query_scale = jnp.repeat(jnp.sqrt(scale_factor), HEAD_SIZE)
    key_clip_scale = jnp.repeat(
        jnp.sqrt(jnp.min(scale_factor.reshape(kv_heads, group_size), axis=1)), HEAD_SIZE
    )
    clipped_query = w_query.astype(jnp.float32) * query_scale[None, :]
    clipped_key = key_projection.astype(jnp.float32) * key_clip_scale[None, :]
    return (
        output,
        input_grad,
        reduced[0],
        reduced[2],
        reduced[3],
        reduced[4],
        reduced[5],
        reduced[1],
        grad_gate,
        grad_up,
        grad_down,
        clipped_query,
        clipped_key,
    )


MESH_IDS = pl.DeviceIdType.MESH
F32 = jnp.float32
BF16 = jnp.bfloat16


class Place:
    def __init__(self, line):
        self.line = line
        self.count = 4 * line
        me = lax.axis_index("dp")
        self.core = lax.axis_index("tensor")
        self.me = me
        self.z = me // 4
        y, x = (me // 2) % 2, me % 2
        self.step_a, self.step_b = 2 - self.core, 1 + self.core
        self.a = y * (1 - self.core) + x * self.core
        self.b = x * (1 - self.core) + y * self.core

    def part(self, z, a, b):
        return z * 4 + a * self.step_a + b * self.step_b

    def up(self):
        return (self.me + 4, self.core)

    def down(self):
        return (self.me - 4, self.core)

    def beside_a(self):
        return (self.me + self.step_a * (1 - 2 * self.a), self.core)

    def beside_b(self):
        return (self.me + self.step_b * (1 - 2 * self.b), self.core)

    def twin(self):
        return (self.me, 1 - self.core)

    def peer(self, offset):
        return lax.rem(self.me + offset, self.count)


def enter(place):
    barrier = pltpu.get_barrier_semaphore()

    def greet(offset, carry):
        pl.semaphore_signal(
            barrier, inc=1, device_id=(place.peer(offset), place.core), device_id_type=MESH_IDS
        )
        return carry

    lax.fori_loop(1, place.count, greet, 0)
    pl.semaphore_signal(barrier, inc=1, device_id=place.twin(), device_id_type=MESH_IDS)
    pl.semaphore_wait(barrier, place.count)


def remote(src, dst, send_sem, recv_sem, device):
    return pltpu.make_async_remote_copy(
        src_ref=src,
        dst_ref=dst,
        send_sem=send_sem,
        recv_sem=recv_sem,
        device_id=device,
        device_id_type=MESH_IDS,
    )


class Notes:
    def __init__(self, place, src, dst, send_sem, recv_sem, alike):
        self.place, self.src, self.dst = place, src, dst
        self.send_sem, self.recv_sem, self.alike = send_sem, recv_sem, alike

    def _copy(self, offset, source):
        place = self.place
        to = place.peer(offset)
        return remote(
            self.src if self.alike else self.src.at[to],
            self.dst.at[source],
            self.send_sem.at[offset],
            self.recv_sem.at[source],
            (to, place.core),
        )

    def start(self):
        def send(offset, carry):
            self._copy(offset, self.place.me).start()
            return carry

        lax.fori_loop(1, self.place.count, send, 0)
        me = self.place.me
        self.dst[me] = self.src[...] if self.alike else self.src[me]

    def finish(self):
        def settle(offset, carry):
            self._copy(offset, self.place.peer(offset)).wait_recv()
            self._copy(offset, self.place.me).wait_send()
            return carry

        lax.fori_loop(1, self.place.count, settle, 0)


class Gather:
    def __init__(self, place, view, send_sem, recv_sem, fixed=False):
        self.place, self.view, self.fixed = place, view, fixed
        self.send_sem, self.recv_sem = send_sem, recv_sem

    def _copy(self, source, target, sem, device):
        there = self.view(source if self.fixed else target)
        return remote(self.view(source), there, self.send_sem.at[sem], self.recv_sem.at[target], device)

    def _to_z(self, z, way):
        place = self.place
        device = place.up() if way == 0 else place.down()
        return self._copy(z, z, way * place.line + z, device)

    def _to_a(self, z):
        line = self.place.line
        return self._copy(z, line + z, 2 * line + z, self.place.beside_a())

    def _to_b(self, slot):
        line = self.place.line
        return self._copy(slot, 2 * line + slot, 3 * line + slot, self.place.beside_b())

    def take(self, slot):
        self._copy(slot, slot, 0, self.place.beside_b()).wait_recv()

    def near(self, step, action):
        place = self.place
        if step == 0:
            action(place.z)
        else:
            pl.when(place.z >= step)(lambda: action(place.z - step))
            pl.when(place.z + step < place.line)(lambda: action(place.z + step))

    def hand_on(self, slot):
        self._to_b(slot).start()

    def start(self):
        place = self.place
        pl.when(place.z < place.line - 1)(lambda: self._to_z(place.z, 0).start())
        pl.when(place.z > 0)(lambda: self._to_z(place.z, 1).start())
        self._to_a(self.place.z).start()
        self.hand_on(self.place.z)

    def along(self, step):
        place = self.place

        def pass_on(z):
            self.take(z)
            pl.when(jnp.logical_and(z < place.z, place.z < place.line - 1))(lambda: self._to_z(z, 0).start())
            pl.when(jnp.logical_and(z > place.z, place.z > 0))(lambda: self._to_z(z, 1).start())
            self._to_a(z).start()
            self.hand_on(z)

        self.near(step, pass_on)

    def across(self, step):
        line = self.place.line

        def pass_on(z):
            self.take(line + z)
            self.hand_on(line + z)

        self.near(step, pass_on)

    def step(self, number):
        if number == 0:
            self.start()
            return
        if number < self.place.line:
            self.along(number)
        self.across(number - 1)

    def settle(self):
        place = self.place
        line = place.line

        def wait(z, carry):
            self._to_a(z).wait_send()
            self._to_b(z).wait_send()
            self._to_b(line + z).wait_send()
            pl.when(jnp.logical_and(z <= place.z, place.z < line - 1))(lambda: self._to_z(z, 0).wait_send())
            pl.when(jnp.logical_and(z >= place.z, place.z > 0))(lambda: self._to_z(z, 1).wait_send())
            return carry

        lax.fori_loop(0, line, wait, 0)

    def take_rest(self):
        line = self.place.line

        def wait(k, carry):
            self.take(2 * line + k)
            return carry

        lax.fori_loop(0, 2 * line, wait, 0)


class Pipeline:
    def __init__(self, gathers, starts):
        self.gathers, self.starts, self.at = gathers, starts, 0
        self.steps = gathers[0].place.line + 1

    def run(self, number):
        for _ in range(number):
            for g, start in zip(self.gathers, self.starts):
                if 0 <= self.at - start < self.steps:
                    g.step(self.at - start)
            self.at += 1

    def until(self, index):
        self.run(max(0, self.starts[index] + self.steps - self.at))


class Twin:
    def __init__(self, place, source, target, send_sem, recv_sem):
        self.place, self.source, self.target = place, source, target
        self.send_sem, self.recv_sem = send_sem, recv_sem

    def copy(self, slot):
        line = self.place.line
        group = slot // line
        there = slot + line * ((group % 2) - (group // 2))
        return remote(
            self.source(slot),
            self.target(there),
            self.send_sem.at[slot],
            self.recv_sem.at[there],
            self.place.twin(),
        )

    def start(self, slot):
        self.copy(slot).start()

    def take(self, slot):
        remote(
            self.source(slot),
            self.target(slot),
            self.send_sem.at[slot],
            self.recv_sem.at[slot],
            self.place.twin(),
        ).wait_recv()

    def wait_send(self, slot):
        self.copy(slot).wait_send()


class Reduce:
    def __init__(self, place, parts, from_b, from_a, from_z, send_sem, recv_sem, index=lambda slot: slot):
        self.place, self.parts, self.index = place, parts, index
        self.from_b, self.from_a, self.from_z = from_b, from_a, from_z
        self.send_sem, self.recv_sem = send_sem, recv_sem

    def _copy(self, source, target, sem, device):
        return remote(source, target, self.send_sem.at[sem], self.recv_sem.at[sem], device)

    def _to_b(self, k):
        line = self.place.line
        return self._copy(self.parts.at[self.index(2 * line + k)], self.from_b.at[k], k, self.place.beside_b())

    def _to_a(self, z):
        line = self.place.line
        block = self.parts.at[self.index(line + z)]
        return self._copy(block, self.from_a.at[z], 2 * line + z, self.place.beside_a())

    def _to_z(self, target):
        place, line = self.place, self.place.line
        return remote(
            self.parts.at[self.index(target)],
            self.from_z.at[place.z],
            self.send_sem.at[3 * line + target],
            self.recv_sem.at[3 * line + place.z],
            (place.me + 4 * (target - place.z), place.core),
        )

    def _add(self, slot, block):
        at = self.index(slot)
        self.parts[at] = (self.parts[at].astype(F32) + block.astype(F32)).astype(BF16)

    def send_b(self, k):
        self._to_b(k).start()

    def fold_b(self, k):
        self._to_b(k).wait_recv()
        self._add(k, self.from_b[k])

    def send_a(self, z):
        self._to_a(z).start()

    def fold_a(self, z):
        self._to_a(z).wait_recv()
        self._add(z, self.from_a[z])

    def fold_line_a(self):
        line = self.place.line
        for z in ends_first(line):
            self.fold_b(line + z)
            self.send_a(z)

    def fold_line_own(self):
        for z in ends_first(self.place.line):
            self.fold_b(z)

    def send_z(self, z):
        pl.when(self.place.z != z)(lambda: self._to_z(z).start())

    def finish_line(self):
        for z in ends_first(self.place.line):
            self.fold_a(z)
            self.send_z(z)

    def result(self, out):
        place, line = self.place, self.place.line
        out[...] = self.parts[self.index(place.z)].astype(F32)

        def add(z, carry):
            @pl.when(z != place.z)
            def _():
                remote(
                    self.from_z.at[z], self.from_z.at[z], self.send_sem.at[0], self.recv_sem.at[3 * line + z], place.up()
                ).wait_recv()
                out[...] += self.from_z[z].astype(F32)

            return carry

        lax.fori_loop(0, line, add, 0)

    def settle_b(self):
        def wait(k, carry):
            self._to_b(k).wait_send()
            return carry

        lax.fori_loop(0, 2 * self.place.line, wait, 0)

    def settle_hop_a(self):
        def wait(z, carry):
            self._to_a(z).wait_send()
            return carry

        lax.fori_loop(0, self.place.line, wait, 0)

    def settle_z(self):
        place = self.place

        def wait(z, carry):
            pl.when(place.z != z)(lambda: self._to_z(z).wait_send())
            return carry

        lax.fori_loop(0, place.line, wait, 0)

    def settle(self):
        self.settle_b()
        self.settle_hop_a()
        self.settle_z()


class PackedGather(Gather):
    def __init__(self, place, dense, packed, compact, picks, mine, send_sem, recv_sem, twin_sems):
        self.place, self.dense, self.packed, self.compact = place, dense, packed, compact
        self.own_pick, self.other_pick = picks
        self.mine, self.fixed = mine, False
        self.send_sem, self.recv_sem = send_sem, recv_sem
        view = lambda slot: compact.at[slot, :, mine]
        self.twin = Twin(place, view, view, twin_sems.at[0], twin_sems.at[1])

    def view(self, slot):
        return self.dense.at[slot]

    def _to_b(self, slot):
        line = self.place.line
        return remote(
            self.packed.at[slot],
            self.compact.at[2 * line + slot, :, self.mine],
            self.send_sem.at[3 * line + slot],
            self.recv_sem.at[2 * line + slot],
            self.place.beside_b(),
        )

    def take_compact(self, slot):
        line = self.place.line
        self._to_b(slot - 2 * line).wait_recv()
        self.twin.start(slot)

    def take(self, slot):
        self._copy(slot, slot, 0, self.place.beside_b()).wait_recv()

    def hand_on(self, slot):
        block = self.dense[slot]
        self.packed[slot] = jnp.dot(self.other_pick[slot], block, preferred_element_type=F32).astype(BF16)
        self._to_b(slot).start()
        self.compact[slot, :, self.mine] = jnp.dot(
            self.own_pick[slot], block, preferred_element_type=F32
        ).astype(BF16)
        self.twin.start(slot)


class PackedReduce(Reduce):
    def __init__(self, place, compact, picks, *rest):
        super().__init__(place, *rest)
        self.compact = compact
        self.own_pick, self.other_pick = picks

    def _to_b(self, k):
        line = self.place.line
        return self._copy(self.compact.at[2 * line + k], self.from_b.at[k], k, self.place.beside_b())

    def fold_b(self, k):
        self._to_b(k).wait_recv()
        own = contract_rows(self.own_pick[k], self.compact[k])
        self.parts[k] = (own + contract_rows(self.other_pick[k], self.from_b[k])).astype(BF16)


def selections(place, notes, own_pick, other_pick, gates=None):
    line = place.line
    cap, length = own_pick.shape[1:]
    rows = [notes[part_of(place, slot)][0:1, :] for slot in range(4 * line)]
    for slot in range(2 * line):
        note = notes[part_of(place, slot)]
        rows.append(jnp.where(place.core == 0, note[3:4, :], note[4:5, :]))
    before = lax.broadcasted_iota(jnp.int32, (length, length), 0) < lax.broadcasted_iota(
        jnp.int32, (length, length), 1
    )
    weights = jnp.concatenate(rows, axis=0)
    rank = jnp.dot(
        jnp.where(weights > 0.0, 1.0, 0.0).astype(BF16),
        jnp.where(before, 1.0, 0.0).astype(BF16),
        preferred_element_type=F32,
    )
    rank = jnp.where(weights > 0.0, rank, -1.0)
    number = lax.broadcasted_iota(jnp.int32, (cap, length), 0).astype(F32)
    for i in range(len(rows)):
        pick = jnp.where(rank[i : i + 1, :] == number, 1.0, 0.0)
        if i >= 4 * line:
            other_pick[i - 4 * line] = pick.astype(BF16)
            continue
        own_pick[i] = pick.astype(BF16)
        if gates is not None:
            gates[cap * i : cap * (i + 1), :] = jnp.sum(pick * rows[i], axis=1, keepdims=True)


AHEAD = 8


class Reductions:
    def __init__(self, reduces, finish):
        self.reduces, self.finish = reduces, finish
        self.at = self.sent = self.limit = 0
        line = self.line = reduces[0].place.line
        self.ks = [line + z for z in ends_first(line)] + ends_first(line)
        self.steps = [(i, k) for i in range(len(reduces)) for k in self.ks]

    def ready(self, number):
        self.limit = 2 * self.line * number
        self._send()

    def _send(self):
        while self.sent < min(self.at + AHEAD, self.limit):
            i, k = self.steps[self.sent]
            self.reduces[i].send_b(k)
            self.sent += 1

    def run(self, number):
        for _ in range(number):
            self._step()

    def _step(self):
        i, k = self.steps[self.at]
        self.at += 1
        self._send()
        self.reduces[i].fold_b(k)
        if k >= self.line:
            self.reduces[i].send_a(k - self.line)
        if k == self.ks[self.line - 1] and i > 0:
            self.reduces[i - 1].finish_line()
        if k == self.ks[-1] and i > 0:
            self.finish(i - 1)

    def complete(self):
        self.run(len(self.steps) - self.at)
        self.reduces[-1].finish_line()
        self.finish(len(self.reduces) - 1)


def reduce_scratch(line, block):
    return [
        pltpu.VMEM((2 * line, *block), BF16),
        pltpu.VMEM((line, *block), BF16),
        pltpu.VMEM((line, *block), BF16),
        pltpu.SemaphoreType.DMA((4 * line,)),
        pltpu.SemaphoreType.DMA((4 * line,)),
    ]


def ends_first(line):
    order = []
    for i in range((line + 1) // 2):
        order += [i] if i == line - 1 - i else [i, line - 1 - i]
    return order


def part_of(place, slot):
    line = place.line
    group, z = slot // line, slot % line
    flip_a, flip_b = group % 2, group // 2
    a = place.a + flip_a * (1 - 2 * place.a)
    b = place.b + flip_b * (1 - 2 * place.b)
    return place.part(z, a, b)


PIECES = 2


def pieces_of(place, width):
    piece = width // 2 // PIECES

    def spans(core):
        starts = [pl.multiple_of((core * PIECES + i) * piece, 128) for i in range(PIECES)]
        return [pl.ds(start, piece) for start in starts]

    return spans(place.core), spans(1 - place.core), piece


def halves(place, width):
    half = width // 2
    mine = pl.ds(pl.multiple_of(place.core * half, 128), half)
    theirs = pl.ds(pl.multiple_of((1 - place.core) * half, 128), half)
    return mine, theirs


def place_half(chunk, have, want, lane):
    chunk = chunk if have == want else pltpu.roll(chunk, HEAD_SIZE, 1)
    return jnp.where(lane // HEAD_SIZE == want, chunk, 0.0)


def rope_chunk(chunk, tables, sign):
    ahead = pltpu.roll(chunk, 128 - HEAD_SIZE // 2, 1)
    behind = pltpu.roll(chunk, HEAD_SIZE // 2, 1)
    return chunk * tables[0] + sign * (ahead * tables[1] + behind * tables[2])


def chunk_of(ref, j):
    return ref[:, 128 * j : 128 * (j + 1)]


def pair_of(ref, j, group_size, lane):
    both = []
    for half in (0, 1):
        group = (2 * j + half) // group_size
        both.append(place_half(chunk_of(ref, group // 2).astype(F32), group % 2, half, lane))
    return jnp.concatenate(both, axis=0).astype(BF16)


def spread_gains(notes, shard, width):
    total = jnp.zeros((8, width), F32)
    for p in range(notes.shape[0]):
        row = jnp.concatenate([notes[p], jnp.zeros((8, width - 128), F32)], axis=1)
        total += pltpu.roll(row, shard * p, 1) if p else row
    return total


def gate_table(logits, ids, experts):
    expo = jnp.exp(logits - jnp.max(logits, axis=0, keepdims=True))
    probs = expo / jnp.sum(expo, axis=0, keepdims=True)
    top, length = logits.shape
    expert = lax.broadcasted_iota(jnp.int32, (experts, length), 0)
    table = jnp.zeros((experts, length), F32)
    for c in range(top):
        table += jnp.where(ids[c : c + 1, :] == expert, probs[c : c + 1, :], 0.0)
    return table


def write_notes(note_ref, gates, gains):
    shard = gains[0].shape[1]
    row = lax.broadcasted_iota(jnp.int32, (8, 128), 0)
    pad = jnp.zeros((1, 128 - shard), F32)
    shared = jnp.zeros((8, 128), F32)
    for i, gain in enumerate(gains):
        shared = jnp.where(row == i + 1, jnp.concatenate([gain, pad], axis=1), shared)
    for p in range(note_ref.shape[0]):
        tile = shared
        for at, e in ((0, p), (3, p + 1 - 2 * (p % 2)), (4, p + 2 - 4 * (p // 2 % 2))):
            tile = jnp.where(row == at, gates[e : e + 1, :], tile)
        note_ref[p] = tile


def tree_tables(segments, parents, length):
    row = lax.broadcasted_iota(jnp.int32, (length, length), 0)
    lane = lax.broadcasted_iota(jnp.int32, (length, length), 1)

    def total(x):
        return jnp.sum(x.astype(F32), axis=1, keepdims=True)

    own_row = segments.astype(F32)
    own = total(jnp.where(row == lane, own_row, 0.0))
    kinds = parents.shape[1]
    kind = lax.broadcasted_iota(jnp.int32, (length, kinds), 1).astype(F32)
    above = parents.astype(F32)
    parent = total(jnp.where(kind == own, above, 0.0))
    grand = total(jnp.where(kind == parent, above, 0.0))
    in_parent, in_grand = own_row == parent, own_row == grand
    start = total(jnp.where(own_row < own, 1.0, 0.0))
    offset = jnp.where(own != 0.0, total(jnp.where(in_parent, 1.0, 0.0)), 0.0)
    offset += jnp.where(parent != 0.0, total(jnp.where(in_grand, 1.0, 0.0)), 0.0)
    place = lax.broadcasted_iota(jnp.int32, (length, 1), 0).astype(F32)
    linked = jnp.logical_or(own_row == own, jnp.logical_or(in_parent, in_grand))
    return place - start + offset, jnp.logical_and(linked, lane <= row)


def write_tables(tables_ref, position):
    lane = lax.broadcasted_iota(jnp.int32, (1, 128), 1)
    half = HEAD_SIZE // 2
    frequency = THETA ** ((lane % half).astype(F32) * (-2.0 / HEAD_SIZE))
    angles = position * frequency
    sine = jnp.sin(angles)
    first = lane % HEAD_SIZE < half
    tables_ref[0] = jnp.cos(angles)
    tables_ref[1] = jnp.where(first, -sine, 0.0)
    tables_ref[2] = jnp.where(first, 0.0, sine)


def forward_part(
    place,
    group_size,
    tokens_ref,
    query_ref,
    key_ref,
    value_ref,
    out_ref,
    cot_ref,
    gain_a_ref,
    gain_m_ref,
    logits_ref,
    ids_ref,
    segments_ref,
    parents_ref,
    moe_in_ref,
    hidden_ref,
    normed_ref,
    head_out_ref,
    queries_ref,
    keys_ref,
    values_ref,
    probs_ref,
    peak_ref,
    tables_ref,
    gains_ref,
    notes,
    query_keep,
    key_keep,
    value_keep,
    out_keep,
    query_all,
    key_all,
    value_all,
    out_all,
    cot_dense,
    cot_packed,
    cot_all,
    own_pick,
    other_pick,
    gates,
    mix_mine,
    mix_other,
    note_ref,
    sends,
    recvs,
    note_send,
    note_recv,
    cot_twins,
    local_sems,
    keep_sems,
    mix_sems,
    kept,
):
    line = place.line
    count = 4 * line
    length, width = tokens_ref.shape
    shard, q_cols = query_ref.shape
    chunks = q_cols // 128
    spans, _, piece = pieces_of(place, width)
    own = []
    blocks = ((query_ref, query_all), (key_ref, key_all), (value_ref, value_all), (out_ref, out_all))
    for i, (src, dst) in enumerate(blocks):
        own.append(pltpu.make_async_copy(src, dst.at[place.me], local_sems.at[i]))
    for i in range(PIECES):
        own.append(pltpu.make_async_copy(cot_ref.at[:, spans[i]], cot_dense.at[i, place.z], local_sems.at[4 + i]))
    for c in own:
        c.start()
    enter(place)
    note = Notes(place, note_ref, notes, note_send, note_recv, False)
    for c in own:
        c.wait()
    gathers = [
        Gather(place, lambda s, ref=ref: ref.at[part_of(place, s)], sends.at[i], recvs.at[i], True)
        for i, ref in enumerate((query_all, key_all, value_all, out_all))
    ]
    picks = (own_pick, other_pick)
    cots = [
        PackedGather(
            place,
            cot_dense.at[i],
            cot_packed.at[i],
            cot_all,
            picks,
            spans[i],
            sends.at[4 + i],
            recvs.at[4 + i],
            cot_twins.at[i],
        )
        for i in range(PIECES)
    ]
    out = gathers[3]
    pipeline = Pipeline([gathers[i] for i in (1, 2, 0, 3)] + cots, STARTS)
    pipeline.run(1)
    gains = [g[...].astype(F32) for g in (gain_a_ref, gain_m_ref)]
    write_notes(note_ref, gate_table(logits_ref[...], ids_ref[...], count), gains)
    note.start()
    inputs = tokens_ref[...].astype(F32)
    inv_attn = lax.rsqrt(jnp.mean(inputs * inputs, axis=1, keepdims=True) + EPSILON)
    pipeline.run(1)
    note.finish()
    gains_ref[...] = spread_gains(notes, shard, width)
    normed_ref[...] = (inputs * inv_attn * gains_ref[1:2, :]).astype(BF16)
    pipeline.run(1)
    position, allowed = tree_tables(segments_ref[...], parents_ref[...], length)
    write_tables(tables_ref, position)
    pipeline.run(1)
    selections(place, notes, own_pick, other_pick, gates)
    pipeline.until(2)
    for g in gathers[:3]:
        g.take_rest()
    normed = normed_ref[...]
    tables = [tables_ref[i] for i in range(3)]
    query_lin = jnp.dot(normed, query_all[...].reshape(width, q_cols), preferred_element_type=F32)
    for j in range(chunks):
        queries_ref[:, 128 * j : 128 * (j + 1)] = rope_chunk(
            query_lin[:, 128 * j : 128 * (j + 1)], tables, 1.0
        ).astype(BF16)
    kv_cols = key_ref.shape[1]
    key_lin = jnp.dot(normed, key_all[...].reshape(width, kv_cols), preferred_element_type=F32)
    for j in range(kv_cols // 128):
        keys_ref[:, 128 * j : 128 * (j + 1)] = rope_chunk(
            key_lin[:, 128 * j : 128 * (j + 1)], tables, 1.0
        ).astype(BF16)
    values_ref[...] = jnp.dot(
        normed, value_all[...].reshape(width, kv_cols), preferred_element_type=F32
    ).astype(BF16)
    lane = lax.broadcasted_iota(jnp.int32, (length, 128), 1)
    small_lane = lax.broadcasted_iota(jnp.int32, (8, 128), 1)
    peaks = jnp.zeros((8, 128), F32)
    pipeline.run(1)
    for j in range(chunks):
        both = contract_cols(chunk_of(queries_ref, j), pair_of(keys_ref, j, group_size, lane)) * SCORE_SCALE
        low = []
        for half in (0, 1):
            scores = jnp.where(allowed, both[:, length * half : length * (half + 1)], NEGATIVE)
            row_max = jnp.max(scores, axis=1, keepdims=True)
            peak = jnp.max(row_max, axis=0, keepdims=True)
            peaks = jnp.where(small_lane == 2 * j + half, peak, peaks)
            expo = jnp.exp(scores - row_max)
            prob = expo / jnp.sum(expo, axis=1, keepdims=True)
            probs_ref[j, :, length * half : length * (half + 1)] = prob
            low.append(prob.astype(BF16))
        mixed = jnp.dot(
            jnp.concatenate(low, axis=1),
            pair_of(values_ref, j, group_size, lane),
            preferred_element_type=F32,
        )
        head_out_ref[:, 128 * j : 128 * (j + 1)] = mixed.astype(BF16)
        pipeline.run(1)
    peak_ref[...] = peaks
    pairs = [(query_all, query_keep), (key_all, key_keep), (value_all, value_keep), *kept[:-1]]
    pairs += [(out_all, out_keep), kept[-1]]
    keeps = [pltpu.make_async_copy(src, dst, keep_sems.at[i]) for i, (src, dst) in enumerate(pairs)]
    for c in keeps[:-2]:
        c.start()
    out.take_rest()
    keeps[-2].start()
    mix_mine[...] = contract_cols(head_out_ref[...], out_all[...].reshape(width, q_cols))
    swap = remote(mix_mine, mix_other, mix_sems.at[0], mix_sems.at[1], place.twin())
    swap.start()
    swap.wait()
    hidden = tokens_ref[...].astype(F32) + RESIDUAL * (mix_mine[...] + mix_other[...])
    hidden_ref[...] = hidden
    keeps[-1].start()
    inv_moe = lax.rsqrt(jnp.mean(hidden * hidden, axis=1, keepdims=True) + EPSILON)
    moe_in_ref[...] = (hidden * inv_moe * gains_ref[2:3, :]).astype(BF16)

    pipeline.until(len(pipeline.gathers) - 1)

    def take_cots():
        def rest(slot, carry):
            for cot in cots:
                cot.take_compact(slot)
            return carry

        lax.fori_loop(2 * line, count, rest, 0)

    def take_twins(group):
        for slot in range(line * group, line * (group + 1)):
            for cot in cots:
                cot.twin.take(slot)
                cot.twin.wait_send(slot)

    def settle():
        for g in gathers + cots:
            g.settle()
        for c in keeps:
            c.wait()

    return take_cots, take_twins, settle


ANY = pl.BlockSpec(memory_space=pl.ANY)
IN_VMEM = pl.BlockSpec(memory_space=pltpu.VMEM)


def params(number):
    return pltpu.CompilerParams(
        collective_id=number, has_side_effects=True, vmem_limit_bytes=60 * 2**20
    )


def capacity_of(length, experts):
    most = 4 * (9 * length * TOP // (32 * experts))
    return min(-(-most // 16) * 16, length)


def experts_part(
    place,
    rows_ref,
    gate_ref,
    up_ref,
    down_ref,
    d_rows_ref,
    mix_ref,
    dense,
    packed,
    rows,
    cots,
    own_pick,
    other_pick,
    gates,
    active,
    d_gate,
    d_up,
    d_active,
    grad_stage,
    mix_stage,
    grad_compact,
    mix_compact,
    grad_dense,
    mix_dense,
    total,
    grad_from_b,
    mix_from_b,
    mix_from_a,
    from_a,
    from_z,
    reduce_sems,
    gather_send,
    gather_recv,
    row_twins,
    last_sems,
    store_sems,
    stored,
    take_cots,
    take_twins,
    settle_before,
):
    line = place.line
    count = 4 * line
    cap, width = rows.shape[1:]
    tile_rows = line * cap
    mine, _ = halves(place, width)
    spans, their_spans, piece = pieces_of(place, width)
    for i in range(PIECES):
        dense[i, place.z] = rows_ref[:, spans[i]]
    picks = (own_pick, other_pick)
    gathers = [
        PackedGather(
            place,
            dense.at[i],
            packed.at[i],
            rows,
            picks,
            spans[i],
            gather_send.at[i],
            gather_recv.at[i],
            row_twins.at[i],
        )
        for i in range(PIECES)
    ]
    grad_twins = [
        Twin(
            place,
            lambda s, i=i: grad_stage.at[s, :, their_spans[i]],
            lambda s, i=i: grad_compact.at[i, s],
            row_twins.at[PIECES + i, 0],
            row_twins.at[PIECES + i, 1],
        )
        for i in range(PIECES)
    ]
    mix_twin = Twin(
        place,
        lambda s: mix_stage.at[s, :, halves(place, width)[1]],
        lambda s: mix_compact.at[s],
        row_twins.at[2 * PIECES, 0],
        row_twins.at[2 * PIECES, 1],
    )
    reduces = [
        PackedReduce(
            place,
            grad_compact.at[i],
            picks,
            grad_dense.at[i],
            grad_from_b.at[i],
            from_a.at[i],
            from_z.at[i],
            reduce_sems.at[i, 0],
            reduce_sems.at[i, 1],
        )
        for i in range(PIECES)
    ]
    mix_reduce = PackedReduce(
        place,
        mix_compact,
        picks,
        mix_dense,
        mix_from_b,
        mix_from_a,
        None,
        reduce_sems.at[PIECES, 0],
        reduce_sems.at[PIECES, 1],
    )

    def group_of(group):
        first = pl.multiple_of(tile_rows * group, tile_rows)
        return pl.ds(line * group, line), pl.ds(first, tile_rows)

    def slots_of(group):
        return [line * group + z for z in range(line)]

    def ahead(group):
        some, flat = group_of(group)
        cot = cots[some].reshape(tile_rows, width).astype(F32)
        d_out = (gates[flat, :] * (RESIDUAL * cot)).astype(BF16)
        cots[some] = d_out.reshape(line, cap, width)
        d_active[flat, :] = jnp.dot(d_out, down_ref[...], preferred_element_type=F32)

    def work(group):
        some, flat = group_of(group)
        for slot in slots_of(group):
            for g in gathers:
                g.twin.take(slot)
        x = rows[some].reshape(tile_rows, width)
        gate_pre = jnp.dot(x, gate_ref[...], preferred_element_type=F32)
        up_pre = jnp.dot(x, up_ref[...], preferred_element_type=F32)
        sigmoid = 1.0 / (1.0 + jnp.exp(-gate_pre))
        silu = gate_pre * sigmoid
        active[flat, :] = (silu * up_pre).astype(BF16)
        d_act = d_active[flat, :]
        d_g = (d_act * up_pre * sigmoid * (1.0 + gate_pre * (1.0 - sigmoid))).astype(BF16)
        d_u = (d_act * silu).astype(BF16)
        d_gate[flat, :] = d_g
        d_up[flat, :] = d_u
        d_in = contract_cols(d_g, gate_ref[...]) + contract_cols(d_u, up_ref[...])
        grad_stage[some] = d_in.astype(BF16).reshape(line, cap, width)
        for twin in grad_twins:
            for slot in slots_of(group):
                twin.start(slot)

    def mix_work(group):
        some, flat = group_of(group)
        mix = gates[flat, :] * contract_cols(active[flat, :], down_ref[...])
        mix_stage[some] = mix.astype(BF16).reshape(line, cap, width)
        for slot in slots_of(group):
            mix_twin.start(slot)

    def fold(twin, stage, span, compact, group, send=None):
        def one(slot, carry):
            twin.take(slot)
            compact[slot] = (compact[slot].astype(F32) + stage[slot, :, span].astype(F32)).astype(BF16)
            if send is not None:
                send(slot - 2 * line)
            return carry

        lax.fori_loop(line * group, line * (group + 1), one, 0)

    def grad_fold(i, group, send=False):
        to_b = reduces[i].send_b if send else None
        fold(grad_twins[i], grad_stage, spans[i], grad_compact.at[i], group, to_b)

    def take_group(group):
        for slot in slots_of(group):
            for g in gathers:
                g.take_compact(slot)

    stores = []
    mix_fold = functools.partial(fold, mix_twin, mix_stage, mine, mix_compact)
    pipeline = Pipeline(gathers, [0] * PIECES)
    pipeline.run(1)
    take_cots()
    pipeline.run(2)
    for group in range(4):
        take_twins(group)

    def ahead_loop(group, carry):
        ahead(group)
        return carry

    lax.fori_loop(0, 4, ahead_loop, 0)
    pipeline.run(2)
    pipeline.until(PIECES - 1)
    work(0)
    take_group(2)
    work(2)
    work(1)
    take_group(3)
    order = ends_first(line)
    grad_fold(0, 2, True)
    for i in range(1, PIECES):
        grad_fold(i, 2)
    work(3)
    for i, (source, target) in enumerate(stored):
        stores.append(pltpu.make_async_copy(source, target, store_sems.at[i]))
        stores[-1].start()
    grad_fold(0, 3, True)
    for i in range(1, PIECES):
        for z in range(line):
            reduces[i].send_b(z)
        grad_fold(i, 3, True)
    mix_work(1)
    for i in range(PIECES):
        grad_fold(i, 1)
    mix_work(2)
    mix_fold(2, mix_reduce.send_b)
    for i in range(PIECES):
        grad_fold(i, 0)
    fillers = [
        lambda: mix_work(3),
        lambda: mix_fold(3, mix_reduce.send_b),
        lambda: mix_work(0),
        lambda: mix_fold(1),
        lambda: mix_fold(0),
    ]
    for i, r in enumerate(reduces):
        for z in order:
            r.fold_b(line + z)
            r.send_a(z)
        if fillers:
            fillers.pop(0)()
        for z in order:
            r.fold_b(z)
        if i > 0:
            reduces[i - 1].finish_line()
        if fillers:
            fillers.pop(0)()
    reduces[-1].finish_line()
    for filler in fillers:
        filler()
    for z in order:
        mix_reduce.fold_b(line + z)
        mix_reduce.send_a(z)
    for z in order:
        mix_reduce.fold_b(z)
    lasts = []
    for i, r in enumerate(reduces):
        r.result(total.at[i])
        d_rows_ref[:, spans[i]] = total[i]
        there = d_rows_ref.at[:, spans[i]]
        lasts.append(remote(total.at[i], there, last_sems.at[0, i], last_sems.at[1, i], place.twin()))
        lasts[-1].start()
    for z in order:
        mix_reduce.fold_a(z)
    stores.append(pltpu.make_async_copy(mix_dense.at[pl.ds(0, line)], mix_ref, store_sems.at[len(stored)]))
    stores[-1].start()
    for r in reduces:
        r.settle()
    mix_reduce.settle_b()
    mix_reduce.settle_hop_a()
    for g in gathers:
        g.settle()

    twins = [g.twin for g in gathers] + grad_twins + [mix_twin]

    def settle(slot, carry):
        for twin in twins:
            twin.wait_send(slot)
        return carry

    lax.fori_loop(0, count, settle, 0)
    for c in stores + lasts:
        c.wait()
    settle_before()


STARTS = (0, 1, 2, 3, 4, 5)
STARTS = (0, 1, 2, 3, 4, 5)


def taken(function, found):
    code = function.__code__
    return {name: found[name] for name in code.co_varnames[: code.co_argcount] if name in found}


def front_kernel(line, group_size, names, *refs):
    found = dict(zip(names, refs))
    r = types.SimpleNamespace(**found)
    place = Place(line)
    sources = (r.gate_hbm, r.up_hbm, r.down_hbm)
    loads = [
        pltpu.make_async_copy(source.at[0], target, r.load_sems.at[i])
        for i, (source, target) in enumerate(zip(sources, (r.gate_ref, r.up_ref, r.down_ref)))
    ]
    for c in loads:
        c.start()
    kept = (
        (r.normed_ref, r.normed_out),
        (r.head_out_ref, r.head_out_out),
        (r.queries_ref, r.queries_out),
        (r.keys_ref, r.keys_out),
        (r.values_ref, r.values_out),
        (r.probs_ref, r.probs_out),
        (r.hidden_ref, r.hidden_out),
    )
    rest = forward_part(place, group_size, kept=kept, **taken(forward_part, found))
    for c in loads:
        c.wait()
    stored = (
        (r.rows, r.rows_out),
        (r.cot_all, r.cots_out),
        (r.active, r.active_out),
        (r.d_gate, r.d_gate_out),
        (r.d_up, r.d_up_out),
    )
    experts_part(
        place,
        r.moe_in_ref,
        cots=r.cot_all,
        stored=stored,
        take_cots=rest[0],
        take_twins=rest[1],
        settle_before=rest[2],
        **taken(experts_part, found),
    )


def run_front(line, group_size, big, small, expert_weights):
    count = 4 * line
    tokens, query, key, value, out, cotangent = big
    length, width = tokens.shape
    q_cols, kv_cols = query.shape[1], key.shape[1]
    hidden = expert_weights[0].shape[2]
    half, cap = width // 2, capacity_of(length, count)
    piece, lines = half // PIECES, 2 * line
    inputs = dict(
        tokens_ref=(tokens, IN_VMEM),
        query_ref=(query, ANY),
        key_ref=(key, ANY),
        value_ref=(value, ANY),
        out_ref=(out, ANY),
        cot_ref=(cotangent, ANY),
        gain_a_ref=(small[0], IN_VMEM),
        gain_m_ref=(small[1], IN_VMEM),
        logits_ref=(small[2], IN_VMEM),
        ids_ref=(small[3], IN_VMEM),
        segments_ref=(small[4], IN_VMEM),
        parents_ref=(small[5], IN_VMEM),
        gate_hbm=(expert_weights[0], ANY),
        up_hbm=(expert_weights[1], ANY),
        down_hbm=(expert_weights[2], ANY),
    )
    rows, inner = (length, width), (count * cap, hidden)
    probs = (q_cols // 128, length, 2 * length)
    outputs = dict(
        hidden_out=(rows, F32, ANY),
        normed_out=(rows, BF16, ANY),
        head_out_out=((length, q_cols), BF16, ANY),
        queries_out=((length, q_cols), BF16, ANY),
        keys_out=((length, kv_cols), BF16, ANY),
        values_out=((length, kv_cols), BF16, ANY),
        probs_out=(probs, F32, ANY),
        peak_ref=((8, 128), F32, IN_VMEM),
        tables_ref=((3, length, 128), F32, IN_VMEM),
        gains_ref=((8, width), F32, IN_VMEM),
        query_keep=((count, *query.shape), BF16, ANY),
        key_keep=((count, *key.shape), BF16, ANY),
        value_keep=((count, *value.shape), BF16, ANY),
        out_keep=((count, *out.shape), BF16, ANY),
        d_rows_ref=(rows, F32, IN_VMEM),
        mix_ref=((line, length, half), BF16, ANY),
        rows_out=((count, cap, width), BF16, ANY),
        cots_out=((count, cap, width), BF16, ANY),
        active_out=(inner, BF16, ANY),
        d_gate_out=(inner, BF16, ANY),
        d_up_out=(inner, BF16, ANY),
    )
    vmem, dma = pltpu.VMEM, pltpu.SemaphoreType.DMA
    dense = vmem((PIECES, lines, length, piece), BF16)
    packed = vmem((PIECES, lines, cap, piece), BF16)
    one_line = vmem((PIECES, line, length, piece), BF16)
    compact = vmem((count, cap, width), BF16)
    scratch = dict(
        hidden_ref=vmem(rows, F32),
        normed_ref=vmem(rows, BF16),
        head_out_ref=vmem((length, q_cols), BF16),
        queries_ref=vmem((length, q_cols), BF16),
        keys_ref=vmem((length, kv_cols), BF16),
        values_ref=vmem((length, kv_cols), BF16),
        probs_ref=vmem(probs, F32),
        query_all=vmem((count, *query.shape), BF16),
        key_all=vmem((count, *key.shape), BF16),
        value_all=vmem((count, *value.shape), BF16),
        out_all=vmem((count, *out.shape), BF16),
        moe_in_ref=vmem(rows, BF16),
        notes=vmem((count, 8, 128), F32),
        note_ref=vmem((count, 8, 128), F32),
        cot_dense=dense,
        cot_packed=packed,
        cot_all=compact,
        own_pick=vmem((count, cap, length), BF16),
        other_pick=vmem((lines, cap, length), BF16),
        gates=vmem((count * cap, 1), F32),
        mix_mine=vmem(rows, F32),
        mix_other=vmem(rows, F32),
        dense=dense,
        packed=packed,
        rows=compact,
        active=vmem(inner, BF16),
        d_gate=vmem(inner, BF16),
        d_up=vmem(inner, BF16),
        d_active=vmem(inner, F32),
        grad_stage=compact,
        mix_stage=compact,
        grad_compact=vmem((PIECES, count, cap, piece), BF16),
        mix_compact=vmem((count, cap, half), BF16),
        grad_dense=dense,
        mix_dense=vmem((lines, length, half), BF16),
        total=vmem((PIECES, length, piece), F32),
        grad_from_b=packed,
        mix_from_b=vmem((lines, cap, half), BF16),
        mix_from_a=vmem((line, length, half), BF16),
        from_a=one_line,
        from_z=one_line,
        gate_ref=vmem((width, hidden), BF16),
        up_ref=vmem((width, hidden), BF16),
        down_ref=vmem((width, hidden), BF16),
        sends=dma((4 + PIECES, 5 * line)),
        recvs=dma((4 + PIECES, count)),
        note_send=dma((count,)),
        note_recv=dma((count,)),
        cot_twins=dma((PIECES, 2, count)),
        local_sems=dma((4 + PIECES,)),
        keep_sems=dma((11,)),
        mix_sems=dma((2,)),
        load_sems=dma((3,)),
        reduce_sems=dma((PIECES + 1, 2, 4 * line)),
        gather_send=dma((PIECES, 5 * line)),
        gather_recv=dma((PIECES, count)),
        row_twins=dma((2 * PIECES + 1, 2, count)),
        last_sems=dma((2, PIECES)),
        store_sems=dma((6,)),
    )
    names = [*inputs, *outputs, *scratch]
    results = pl.pallas_call(
        functools.partial(front_kernel, line, group_size, names),
        out_shape=[jax.ShapeDtypeStruct(shape, kind) for shape, kind, _ in outputs.values()],
        in_specs=[spec for _, spec in inputs.values()],
        out_specs=[spec for _, _, spec in outputs.values()],
        scratch_shapes=list(scratch.values()),
        compiler_params=params(0),
        name="run_front",
    )(*(x for x, _ in inputs.values()))
    return types.SimpleNamespace(**dict(zip(outputs, results)))


def backward_kernel(
    line,
    group_size,
    tokens_ref,
    hidden_ref,
    d_rows_ref,
    cot_ref,
    normed_ref,
    head_out_ref,
    queries_ref,
    keys_ref,
    values_ref,
    probs_ref,
    gains_ref,
    peak_ref,
    tables_ref,
    query_keep,
    key_keep,
    value_keep,
    out_keep,
    mix_ref,
    rows_hbm,
    cots_hbm,
    active_hbm,
    d_gate_hbm,
    d_up_hbm,
    input_grad_ref,
    output_ref,
    query_sum,
    key_sum,
    value_sum,
    out_sum,
    notes,
    grad_gate_ref,
    grad_up_ref,
    grad_down_ref,
    *scratch,
):
    place = Place(line)
    count = 4 * line
    length, width = tokens_ref.shape
    q_cols, kv_cols = queries_ref.shape[1], keys_ref.shape[1]
    shard = width // count
    chunks = q_cols // 128
    (query_all, key_all, value_all, out_all), work = scratch[:4], scratch[4:9]
    rest = scratch[9:34]
    (
        total,
        d_heads,
        d_query,
        d_key,
        d_value,
        part_mine,
        part_other,
        d_hidden_keep,
        mix_total,
        note,
        weight_sems,
        load_sems,
        last_sems,
        part_sems,
        note_sends,
        note_recvs,
        expert_rows,
        cots,
        active,
        d_gate,
        d_up,
        grads,
        expert_sems,
        store_sems,
    ) = scratch[34:]
    by_part = lambda slot: part_of(place, slot)
    reduces = [
        Reduce(place, work[i], *rest[5 * i : 5 * i + 5], *(() if i == 4 else (by_part,))) for i in range(5)
    ]

    def load(slot):
        return pltpu.make_async_copy(mix_ref.at[slot], work[4].at[slot], load_sems.at[slot])

    def begin(slot, carry):
        load(slot).start()
        return carry

    def loaded(slot, carry):
        load(slot).wait()
        return carry

    lax.fori_loop(0, line, begin, 0)
    weights = [
        pltpu.make_async_copy(src, dst, weight_sems.at[i])
        for i, (src, dst) in enumerate(
            ((out_keep, out_all), (query_keep, query_all), (key_keep, key_all), (value_keep, value_all))
        )
    ]
    for c in weights:
        c.start()
    experts = [
        pltpu.make_async_copy(src, dst, expert_sems.at[i])
        for i, (src, dst) in enumerate(
            ((rows_hbm, expert_rows), (cots_hbm, cots), (active_hbm, active), (d_gate_hbm, d_gate), (d_up_hbm, d_up))
        )
    ]
    for c in experts:
        c.start()
    stores = [
        pltpu.make_async_copy(grads.at[i], dst, store_sems.at[i])
        for i, dst in enumerate((grad_gate_ref, grad_up_ref, grad_down_ref))
    ]
    columns = width // 512

    def weight_grad(number):
        left, right = ((expert_rows, d_gate), (expert_rows, d_up), (cots, active))[number]
        left = left.reshape(left.shape[0] * left.shape[1], width)

        def some(i, carry):
            span = pl.ds(pl.multiple_of(512 * i, 512), 512)
            grads[number, span, :] = contract_rows(left[:, span], right[...])
            return carry

        lax.fori_loop(0, columns, some, 0)
        stores[number].start()

    enter(place)
    lax.fori_loop(0, line, loaded, 0)
    mine, theirs = halves(place, width)
    outs = (query_sum, key_sum, value_sum, out_sum, total)
    order = (3, 0, 1, 2)
    mix = reduces[4]
    for z in ends_first(line):
        mix.send_z(z)
    last = remote(total, mix_total.at[:, mine], last_sems.at[0], last_sems.at[1], place.twin())

    def finish(at):
        i = order[at]
        reduces[i].result(outs[i])

    run = Reductions([reduces[i] for i in order], finish)
    hidden = hidden_ref[...]
    inv_moe = lax.rsqrt(jnp.mean(hidden * hidden, axis=1, keepdims=True) + EPSILON)
    unit_moe = hidden * inv_moe
    d_rows = d_rows_ref[...]
    scaled = d_rows * gains_ref[2:3, :]
    d_hidden = cot_ref[...].astype(F32) + inv_moe * (
        scaled - unit_moe * jnp.mean(scaled * unit_moe, axis=1, keepdims=True)
    )
    d_hidden_keep[...] = d_hidden
    moe_gain = jnp.sum(d_rows * unit_moe, axis=0, keepdims=True)
    d_attn = (RESIDUAL * d_hidden).astype(BF16)
    work[3][...] = contract_rows(d_attn, head_out_ref[...]).astype(BF16).reshape(count, shard, q_cols)
    run.ready(1)
    weights[0].wait()
    d_heads[...] = jnp.dot(
        d_attn, out_all[...].reshape(width, q_cols), preferred_element_type=F32
    ).astype(BF16)
    lane = lax.broadcasted_iota(jnp.int32, (length, 128), 1)
    d_key[...] = jnp.zeros_like(d_key)
    d_value[...] = jnp.zeros_like(d_value)
    tables = [tables_ref[i] for i in range(3)]
    for j in range(chunks):
        d_out = chunk_of(d_heads, j)
        keys = pair_of(keys_ref, j, group_size, lane)
        d_prob = contract_cols(d_out, pair_of(values_ref, j, group_size, lane))
        low, d_scores = [], []
        for half in (0, 1):
            side = slice(length * half, length * (half + 1))
            prob = probs_ref[j, :, side]
            grad = d_prob[:, side]
            inner = jnp.sum(prob * grad, axis=1, keepdims=True)
            d_scores.append((prob * (grad - inner)).astype(BF16))
            low.append(prob.astype(BF16))
        d_scores = jnp.concatenate(d_scores, axis=1)
        d_values = contract_rows(jnp.concatenate(low, axis=1), d_out)
        d_keys = contract_rows(d_scores, chunk_of(queries_ref, j)) * SCORE_SCALE
        turned = rope_chunk(
            jnp.dot(d_scores, keys, preferred_element_type=F32) * SCORE_SCALE, tables, -1.0
        )
        d_query[:, 128 * j : 128 * (j + 1)] = turned.astype(BF16)
        for half in (0, 1):
            group = (2 * j + half) // group_size
            side = slice(length * half, length * (half + 1))
            cols = slice(128 * (group // 2), 128 * (group // 2 + 1))
            d_key[:, cols] += place_half(d_keys[side], half, group % 2, lane)
            d_value[:, cols] += place_half(d_values[side], half, group % 2, lane)
        run.run(1)
    normed = normed_ref[...]
    work[0][...] = contract_rows(normed, d_query[...]).astype(BF16).reshape(count, shard, q_cols)
    run.ready(2)
    d_key_lin = jnp.concatenate(
        [rope_chunk(chunk_of(d_key, j), tables, -1.0) for j in range(kv_cols // 128)], axis=1
    ).astype(BF16)
    d_value_lin = d_value[...].astype(BF16)
    run.run(2)
    work[1][...] = contract_rows(normed, d_key_lin).astype(BF16).reshape(count, shard, kv_cols)
    work[2][...] = contract_rows(normed, d_value_lin).astype(BF16).reshape(count, shard, kv_cols)
    run.ready(4)
    run.run(2)
    mix.result(total)
    mix_total[:, mine] = total[...]
    last.start()
    for c in weights[1:]:
        c.wait()
    part_mine[...] = (
        contract_cols(d_query[...], query_all[...].reshape(width, q_cols))
        + contract_cols(d_key_lin, key_all[...].reshape(width, kv_cols))
        + contract_cols(d_value_lin, value_all[...].reshape(width, kv_cols))
    )
    swap = remote(part_mine, part_other, part_sems.at[0], part_sems.at[1], place.twin())
    swap.start()
    run.run(4)
    swap.wait()
    d_normed = part_mine[...] + part_other[...]
    inputs = tokens_ref[...].astype(F32)
    inv_attn = lax.rsqrt(jnp.mean(inputs * inputs, axis=1, keepdims=True) + EPSILON)
    unit_attn = inputs * inv_attn
    scaled = d_normed * gains_ref[1:2, :]
    input_grad_ref[...] = d_hidden_keep[...] + inv_attn * (
        scaled - unit_attn * jnp.mean(scaled * unit_attn, axis=1, keepdims=True)
    )
    attn_gain = jnp.sum(d_normed * unit_attn, axis=0, keepdims=True)
    rows = jnp.concatenate([attn_gain, moe_gain, jnp.zeros((6, width), F32)], axis=0)
    row = lax.broadcasted_iota(jnp.int32, (8, 128), 0)
    peaks = jnp.broadcast_to(peak_ref[0:1, :], (8, 128))
    for p in range(count):
        turned = pltpu.roll(rows, width - shard * p, 1) if p else rows
        note[p] = jnp.where(row == 2, peaks, turned[:, :128])
    exchange = Notes(place, note, notes, note_sends, note_recvs, False)
    exchange.start()
    for c in experts:
        c.wait()
    for number in range(3):
        weight_grad(number)
        run.run(6)
    run.complete()
    for r in reduces[:4]:
        r.settle()
    mix.settle_z()
    last.wait()
    output_ref[...] = (hidden_ref[...] + RESIDUAL * mix_total[...]).astype(BF16)
    exchange.finish()
    for c in stores:
        c.wait()


def run_backward(line, group_size, kept, keeps, mix, experts):
    count = 4 * line
    tokens, queries, keys = kept[0], kept[6], kept[7]
    length, width = tokens.shape
    q_cols, kv_cols = queries.shape[1], keys.shape[1]
    blocks = [x.shape[1:] for x in keeps] + [mix.shape[1:]]
    half = width // 2
    shape = jax.ShapeDtypeStruct
    outs = (
        [shape((length, width), F32), shape((length, width), BF16)]
        + [shape(s, F32) for s in blocks[:4]]
        + [shape((count, 8, 128), F32)]
    )
    kinds = [IN_VMEM] * len(outs) + [ANY] * 3
    hidden = experts[2].shape[1]
    outs += [shape((width, hidden), F32)] * 3
    return pl.pallas_call(
        functools.partial(backward_kernel, line, group_size),
        out_shape=outs,
        in_specs=[IN_VMEM] * len(kept) + [ANY] * 10,
        out_specs=kinds,
        scratch_shapes=[pltpu.VMEM(x.shape, BF16) for x in keeps]
        + [pltpu.VMEM((count, *s), BF16) for s in blocks[:4]]
        + [pltpu.VMEM(mix.shape, BF16)]
        + [x for s in blocks for x in reduce_scratch(line, s)]
        + [
            pltpu.VMEM((length, half), F32),
            pltpu.VMEM((length, q_cols), BF16),
            pltpu.VMEM((length, q_cols), BF16),
            pltpu.VMEM((length, kv_cols), F32),
            pltpu.VMEM((length, kv_cols), F32),
            pltpu.VMEM((length, width), F32),
            pltpu.VMEM((length, width), F32),
            pltpu.VMEM((length, width), F32),
            pltpu.VMEM((length, width), F32),
            pltpu.VMEM((count, 8, 128), F32),
            pltpu.SemaphoreType.DMA((4,)),
            pltpu.SemaphoreType.DMA((count,)),
            pltpu.SemaphoreType.DMA((2,)),
            pltpu.SemaphoreType.DMA((2,)),
            pltpu.SemaphoreType.DMA((count,)),
            pltpu.SemaphoreType.DMA((count,)),
        ]
        + [pltpu.VMEM(x.shape, BF16) for x in experts]
        + [
            pltpu.VMEM((3, width, hidden), F32),
            pltpu.SemaphoreType.DMA((5,)),
            pltpu.SemaphoreType.DMA((3,)),
        ],
        compiler_params=params(3),
        name="run_backward",
    )(*kept, *keeps, mix, *experts)


def finish_kernel(
    group_size,
    output_in,
    input_grad_in,
    query_in,
    key_in,
    value_in,
    out_in,
    notes,
    query_ref,
    key_ref,
    gate_in,
    up_in,
    down_in,
    output,
    input_grad,
    grad_query,
    grad_key,
    grad_value,
    grad_out,
    gain_a,
    gain_m,
    clipped_query,
    clipped_key,
    grad_gate,
    grad_up,
    grad_down,
    stage,
    sems,
):
    pairs = ((gate_in, grad_gate), (up_in, grad_up), (down_in, grad_down))
    takes = [pltpu.make_async_copy(src, stage.at[i], sems.at[0, i]) for i, (src, _) in enumerate(pairs)]
    copies = [pltpu.make_async_copy(stage.at[i], dst.at[0], sems.at[1, i]) for i, (_, dst) in enumerate(pairs)]
    for c in takes:
        c.start()
    output[...] = output_in[...]
    input_grad[...] = input_grad_in[...]
    grad_query[...] = query_in[...]
    grad_key[...] = key_in[...]
    grad_value[...] = value_in[...]
    grad_out[...] = out_in[...]
    for take, c in zip(takes, copies):
        take.wait()
        c.start()
    total, peaks = notes[0], notes[0]
    for p in range(1, notes.shape[0]):
        total = total + notes[p]
        peaks = jnp.maximum(peaks, notes[p])
    shard = gain_a.shape[1]
    gain_a[...] = total[0:1, :shard]
    gain_m[...] = total[1:2, :shard]
    factor = CLIP_LIMIT / jnp.maximum(peaks, CLIP_LIMIT)
    root = jnp.sqrt(factor)
    lane = lax.broadcasted_iota(jnp.int32, (8, 128), 1)

    def scale(h):
        return jnp.max(jnp.where(lane == h, root, 0.0), axis=1, keepdims=True)[2:3, :]

    heads = query_ref.shape[1] // HEAD_SIZE
    wide = lax.broadcasted_iota(jnp.int32, (1, 128), 1)
    scales = [scale(h) for h in range(heads)]
    for j in range(heads // 2):
        row = jnp.where(wide < HEAD_SIZE, scales[2 * j], scales[2 * j + 1])
        cols = slice(128 * j, 128 * (j + 1))
        clipped_query[:, cols] = query_ref[:, cols].astype(F32) * row
    least = [
        functools.reduce(jnp.minimum, scales[group_size * g : group_size * (g + 1)])
        for g in range(heads // group_size)
    ]
    for j in range(len(least) // 2):
        row = jnp.where(wide < HEAD_SIZE, least[2 * j], least[2 * j + 1])
        cols = slice(128 * j, 128 * (j + 1))
        clipped_key[:, cols] = key_ref[:, cols].astype(F32) * row
    for c in copies:
        c.wait()


def finish(group_size, found, notes, query, key, expert_grads):
    shape = jax.ShapeDtypeStruct
    shard = query.shape[0]
    outs = [shape(x.shape, x.dtype) for x in found] + [
        shape((1, shard), F32),
        shape((1, shard), F32),
        shape(query.shape, F32),
        shape(key.shape, F32),
    ]
    return pl.pallas_call(
        functools.partial(finish_kernel, group_size),
        out_shape=outs + [shape((1, *g.shape), F32) for g in expert_grads],
        in_specs=[IN_VMEM] * 9 + [ANY] * 3,
        out_specs=[IN_VMEM] * 10 + [ANY] * 3,
        scratch_shapes=[
            pltpu.VMEM((3, *expert_grads[0].shape), F32),
            pltpu.SemaphoreType.DMA((2, 3)),
        ],
        compiler_params=pltpu.CompilerParams(vmem_limit_bytes=56 * 2**20),
        name="finish",
    )(*found, notes, query, key, *expert_grads)


def on_device_dense(
    tokens,
    attn_norm_gain,
    w_query,
    key_projection,
    value_projection,
    w_out,
    moe_norm_gain,
    w_gate,
    w_up,
    w_down,
    router_logits,
    expert_ids,
    segment_ids,
    parents,
    cotangent,
):
    length, model_width = tokens.shape
    q_cols, kv_cols = w_query.shape[1], key_projection.shape[1]
    q_heads, kv_heads = q_cols // HEAD_SIZE, kv_cols // HEAD_SIZE
    group_size = q_heads // kv_heads
    count = lax.axis_size("dp")
    line = count // 4
    shard = attn_norm_gain.shape[0]
    small = (
        attn_norm_gain[None],
        moe_norm_gain[None],
        router_logits.T,
        expert_ids.T,
        segment_ids,
        parents,
    )
    big = (tokens, w_query, key_projection, value_projection, w_out, cotangent)
    front = run_front(line, group_size, big, small, (w_gate, w_up, w_down))
    keeps = (front.query_keep, front.key_keep, front.value_keep, front.out_keep)
    experts = (front.rows_out, front.cots_out, front.active_out, front.d_gate_out, front.d_up_out)
    kept = (
        tokens,
        front.hidden_out,
        front.d_rows_ref,
        cotangent,
        front.normed_out,
        front.head_out_out,
        front.queries_out,
        front.keys_out,
        front.values_out,
        front.probs_out,
        front.gains_ref,
        front.peak_ref,
        front.tables_ref,
    )
    input_grad, output, *grads = run_backward(line, group_size, kept, keeps, front.mix_ref, experts)
    grads, sums, expert_grads = grads[:4], grads[4], grads[5:]
    output, input_grad, gq, gk, gv, go, gain_a, gain_m, clipped_query, clipped_key, gg, gu, gd = finish(
        group_size, (output, input_grad, *grads), sums, w_query, key_projection, expert_grads
    )
    return (
        output,
        input_grad,
        gain_a[0],
        gq,
        gk,
        gv,
        go,
        gain_m[0],
        gg,
        gu,
        gd,
        clipped_query,
        clipped_key,
    )


DENSE_BYTES = 8 * 2**20


def on_device(*args):
    tokens, w_gate = args[0], args[7]
    count, ranks = lax.axis_size("dp"), lax.axis_size("tensor")
    rows_bytes = count * tokens.shape[0] * tokens.shape[1] * 2
    whole_experts = w_gate.shape[2] * ranks == FFE
    dense = whole_experts and ranks == 2 and count % 8 == 0 and rows_bytes <= DENSE_BYTES
    return on_device_dense(*args) if dense else on_device_general(*args)


def solution(mesh):
    in_specs = (
        P("dp", None),
        P("dp"),
        P("dp", "tensor"),
        P("dp", "tensor"),
        P("dp", "tensor"),
        P("dp", "tensor"),
        P("dp"),
        P("dp", None, "tensor"),
        P("dp", None, "tensor"),
        P("dp", None, "tensor"),
        P("dp", None),
        P("dp", None),
        P("dp", None),
        P("dp", None),
        P("dp", None),
    )
    out_specs = (
        P("dp", None),
        P("dp", None),
        P("dp"),
        P("dp", "tensor"),
        P("dp", "tensor"),
        P("dp", "tensor"),
        P("dp", "tensor"),
        P("dp"),
        P("dp", None, "tensor"),
        P("dp", None, "tensor"),
        P("dp", None, "tensor"),
        P("dp", "tensor"),
        P("dp", "tensor"),
    )
    return jax.shard_map(
        on_device, mesh=mesh, in_specs=in_specs, out_specs=out_specs, check_vma=False
    )
```

profile of v0, /device:TPU:0, one launch (start us, length us, event | category | flops | bytes accessed | tf_op | source)
XLA Modules:
  0.0 244.2 jit_solution(8765693110602540558)
XLA Ops:
  0.6 158.3 %run_front.1 = (f32[128,1536]{1,0:T(8,128)}, bf16[128,1536]{1,0:T(8,128)(2,1)}, bf16[128,768]{1,0:T(8,128)(2,1)}, bf16[128,768]{1,0:T(8,128)(2,1)}, bf16[128,256...) custom-call(bf16[128,1536]{1,0:T(8,128)(2,1)} %tokens_ref.1, ...), custom_call_target="tpu_custom_call" | custom-call | tf_op jit(solution)/shard_map/run_front/pallas_call | solution.py:1664
  158.9 78.5 %run_backward.1 = (f32[128,1536]{1,0:T(8,128)}, bf16[128,1536]{1,0:T(8,128)(2,1)}, f32[96,768]{1,0:T(8,128)}, f32[96,256]{1,0:T(8,128)}, f32[96,256]{1,0:T(8,128...) custom-call(bf16[128,1536]{1,0:T(8,128)(2,1)} %tokens_ref.1, ...), custom_call_target="tpu_custom_call" | custom-call | tf_op jit(solution)/shard_map/run_backward/pallas_call | solution.py:1936
  237.5 6.6 %finish.1 = (bf16[128,1536]{1,0:T(8,128)(2,1)}, f32[128,1536]{1,0:T(8,128)}, f32[96,768]{1,0:T(8,128)}, f32[96,256]{1,0:T(8,128)}, f32[96,256]{1,0:T(8,128)}, /*...) custom-call(bf16[128,1536]{1,0:T(8,128)(2,1)} %get-tuple-element.78., ...), custom_call_target="tpu_custom_call" | custom-call | tf_op jit(solution)/shard_map/finish/pallas_call | solution.py:2060
where the time goes:
time: 244 us
  Pallas kernels  243 us (100%)
    pallas_call x1, Pallas kernels, run_front(): pl.pallas_call(functools.partial(front_kernel, line, group_size, names),...  158 us
    pallas_call x1, Pallas kernels, run_backward(): pl.pallas_call(functools.partial(backward_kernel, line, group_size), out_...  78.5 us
    pallas_call x1, Pallas kernels, finish(): pl.pallas_call(functools.partial(finish_kernel, group_size), out_shape=ou...  6.55 us

commit v1 on v0

--- a/solution.py
+++ b/solution.py
@@ -1673,9 +1673,20 @@
     return types.SimpleNamespace(**dict(zip(outputs, results)))
 
 
+def backward_entry(line, group_size, number, *refs):
+    targets, sems = refs[-number - 1 : -1], refs[-1]
+    loads = [
+        pltpu.make_async_copy(src, dst, sems.at[i]) for i, (src, dst) in enumerate(zip(refs[:number], targets))
+    ]
+    for c in loads:
+        c.start()
+    backward_kernel(line, group_size, loads, *targets, *refs[number : -number - 1])
+
+
 def backward_kernel(
     line,
     group_size,
+    loads,
     tokens_ref,
     hidden_ref,
     d_rows_ref,
@@ -1797,6 +1808,8 @@
         stores[number].start()
 
     enter(place)
+    for c in loads:
+        c.wait()
     lax.fori_loop(0, line, loaded, 0)
     mine, theirs = halves(place, width)
     outs = (query_sum, key_sum, value_sum, out_sum, total)
@@ -1934,9 +1947,9 @@
     hidden = experts[2].shape[1]
     outs += [shape((width, hidden), F32)] * 3
     return pl.pallas_call(
-        functools.partial(backward_kernel, line, group_size),
+        functools.partial(backward_entry, line, group_size, len(kept)),
         out_shape=outs,
-        in_specs=[IN_VMEM] * len(kept) + [ANY] * 10,
+        in_specs=[ANY] * (len(kept) + 10),
         out_specs=kinds,
         scratch_shapes=[pltpu.VMEM(x.shape, BF16) for x in keeps]
         + [pltpu.VMEM((count, *s), BF16) for s in blocks[:4]]
@@ -1965,7 +1978,9 @@
             pltpu.VMEM((3, width, hidden), F32),
             pltpu.SemaphoreType.DMA((5,)),
             pltpu.SemaphoreType.DMA((3,)),
-        ],
+        ]
+        + [pltpu.VMEM(x.shape, x.dtype) for x in kept]
+        + [pltpu.SemaphoreType.DMA((len(kept),))],
         compiler_params=params(3),
         name="run_backward",
     )(*kept, *keeps, mix, *experts)

time: 244 us -> 243 us (level)
  no operation moved by 1% of the time
where the time goes in v1:
time: 243 us
  Pallas kernels  242 us (100%)
    pallas_call x1, Pallas kernels, run_front(): pl.pallas_call(functools.partial(front_kernel, line, group_size, names),...  158 us
    pallas_call x1, Pallas kernels, run_backward(): pl.pallas_call(functools.partial(backward_entry, line, group_size, len(ke...  76.9 us
    pallas_call x1, Pallas kernels, finish(): pl.pallas_call(functools.partial(finish_kernel, group_size), out_shape=ou...  6.55 us

profile of v1, /device:TPU:0, one launch (start us, length us, event | category | flops | bytes accessed | tf_op | source)
XLA Modules:
  0.0 242.5 jit_solution(3819377572104023014)
XLA Ops:
  0.6 158.3 %run_front.1 = (f32[128,1536]{1,0:T(8,128)}, bf16[128,1536]{1,0:T(8,128)(2,1)}, bf16[128,768]{1,0:T(8,128)(2,1)}, bf16[128,768]{1,0:T(8,128)(2,1)}, bf16[128,256...) custom-call(bf16[128,1536]{1,0:T(8,128)(2,1)} %refs_0_.3, ...), custom_call_target="tpu_custom_call" | custom-call | tf_op jit(solution)/shard_map/run_front/pallas_call | solution.py:1664
  158.9 76.9 %run_backward.1 = (f32[128,1536]{1,0:T(8,128)}, bf16[128,1536]{1,0:T(8,128)(2,1)}, f32[96,768]{1,0:T(8,128)}, f32[96,256]{1,0:T(8,128)}, f32[96,256]{1,0:T(8,128...) custom-call(bf16[128,1536]{1,0:T(8,128)(2,1)} %refs_0_.3, ...), custom_call_target="tpu_custom_call" | custom-call | tf_op jit(solution)/shard_map/run_backward/pallas_call | solution.py:1949
  235.8 6.6 %finish.1 = (bf16[128,1536]{1,0:T(8,128)(2,1)}, f32[128,1536]{1,0:T(8,128)}, f32[96,768]{1,0:T(8,128)}, f32[96,256]{1,0:T(8,128)}, f32[96,256]{1,0:T(8,128)}, /*...) custom-call(bf16[128,1536]{1,0:T(8,128)(2,1)} %get-tuple-element.78., ...), custom_call_target="tpu_custom_call" | custom-call | tf_op jit(solution)/shard_map/finish/pallas_call | solution.py:2075
